TPU v7x, 32 devices: a whole 2x2x4 slice. The times are simulated.
32 devices in a mesh: section: 4 (over y, core), dp: 8 (over z, x).
Axes of the slice: x: 2, y: 2, z: 4, core: 2. Of those that a mesh axis runs over, the one named last changes fastest.
Arguments:
- fresh_batches: bfloat16 [3, 512, 4096], P(None, 'dp'), may hold values from -6 to 6
- held_states: bfloat16 [4, 512, 4096], P('section', 'dp'), may hold values from -6 to 6
- section_weight: bfloat16 [4, 4096, 4096], P('section', None, 'dp'), may hold values from -0.09375 to 0.09375
- section_gain: float32 [4, 4096], P('section'), may hold values from 0.25 to 1.75
- final_gain: float32 [4096], replicated, may hold values from 0.3 to 3
- cached_pool: bfloat16 [512, 4096], P('dp'), may hold values from -0.09375 to 0.09375
- route: int32 [8, 64], P('dp'), may hold values from 0 to 63, each once within a row
- queries: bfloat16 [256, 4096], P(('section', 'dp')), may hold values from -0.09375 to 0.09375
- shortlist: int32 [256, 128], P(('section', 'dp')), may hold values from 0 to 63
- teacher: float32 [256, 128], P(('section', 'dp')), may hold values from -16 to 300, as said below
Outputs:
- held_out: bfloat16 [4, 512, 4096], P('section', 'dp')
- losses: float32 [256], P(('section', 'dp'))
- query_grad: float32 [256, 4096], P(('section', 'dp'))
- pool_grad: bfloat16 [512, 4096], P('dp')
Inputs may be any that keep to these rules, and one draw needn't show every extreme that they name: `teacher`: reranker scores; on some draws some rows have two entries above the rest.
All inputs are finite; a program needn't handle non-finite values.
Results may differ from a plain program's by a relative error of at most 0.0058.
Values may be sent and summed in bfloat16 or wider, within the bound.
No kernel may reach another device: no remote copies, remote signals or barrier semaphores. Data moves between devices by JAX's collectives and lax.ppermute only.
A program may use at most 64 MiB of HBM per device.

v0:
```python
import jax
import jax.numpy as jnp
from jax import lax
from jax.sharding import PartitionSpec as P

SEQ = 128
TICKS = 3
epsilon = 1e-06
logit_scale = 20.0
AXES = ("section", "dp")


def on_device(
    fresh_batches,
    held_states,
    section_weight,
    section_gain,
    final_gain,
    cached_pool,
    route,
    queries,
    shortlist,
    teacher,
):
    section = lax.axis_index("section")
    sections = lax.axis_size("section")
    dp = lax.axis_index("dp")
    dps = lax.axis_size("dp")
    half = dps // 2
    side, place = (dp % 2, dp // 2)
    weight = section_weight[0]
    gain = section_gain[0]
    width, cols = weight.shape
    tok = held_states.shape[1]
    pair_rows = 2 * tok

    def send(x, hops):
        return lax.ppermute(
            x,
            AXES,
            [(a * dps + i, b * dps + (i ^ flip)) for a, b, flip in hops for i in range(dps)],
        )

    rows = cached_pool.shape[0]
    outbox = jnp.concatenate(
        [
            jnp.take(cached_pool, route[0], axis=0),
            jnp.broadcast_to(route[0].astype(jnp.bfloat16)[:, None], (rows, 128)),
        ],
        axis=1,
    )
    inbox = lax.all_to_all(outbox, "dp", split_axis=0, concat_axis=0, tiled=True)
    owner_queries = lax.all_gather(queries, "section", axis=0, tiled=True)
    gained = (weight.astype(jnp.float32) * gain[:, None]).astype(jnp.bfloat16)
    by_side = gained.reshape(half, 2, cols, cols)
    flips = jnp.where(section == 0, 0, place)
    mine_plain = lax.dynamic_index_in_dim(by_side, side, 1, keepdims=False)
    theirs_plain = lax.dynamic_index_in_dim(by_side, 1 - side, 1, keepdims=False)
    last_full = sections - 1 - TICKS
    theirs_plain = send(theirs_plain, [(a, a, 1) for a in range(sections - 1)])
    order = jnp.arange(half) ^ flips
    inner = half * cols

    def ordered(w):
        return jnp.take(w, order, axis=0).reshape(inner, cols)

    mine_late, theirs_late = (ordered(mine_plain), ordered(theirs_plain))
    if last_full == 0:
        mine_first, theirs_first = (mine_late, theirs_late)
    else:
        mine_first = mine_plain.reshape(inner, cols)
        theirs_first = theirs_plain.reshape(inner, cols)

    def layer(states, mine, theirs, own_at, hops):
        wide = states.astype(jnp.float32)
        square = jnp.sum(wide * wide, axis=-1)
        other_square = send(square, hops)
        other = send(
            jnp.dot(states, theirs, preferred_element_type=jnp.float32).astype(jnp.bfloat16), hops
        )
        own = jnp.dot(states, mine, preferred_element_type=jnp.float32)
        inv_rms = lax.rsqrt((square + other_square) / width + epsilon)
        projected = ((own + other.astype(jnp.float32)) * inv_rms[:, None]).astype(jnp.bfloat16)
        kept = lax.dynamic_slice_in_dim(states, own_at * cols, cols, axis=1).astype(jnp.float32)
        return (kept + jax.nn.silu(projected.astype(jnp.float32))).astype(jnp.bfloat16)

    def token_order(block):
        piled = block.reshape(half, pair_rows, cols)
        return jnp.take(piled, jnp.arange(half) ^ place, axis=0).reshape(block.shape)

    entry = held_states[0]
    for i in range(TICKS - 1):
        entry = jnp.where(section == sections - TICKS + 1 + i, fresh_batches[i], entry)
    used = list(range(last_full + 1)) + list(range(sections - TICKS + 1, sections))
    entry = entry.reshape(tok, half, 2, cols)
    stay = lax.dynamic_index_in_dim(entry, side, 2, keepdims=False).reshape(tok, inner)
    leave = lax.dynamic_index_in_dim(entry, 1 - side, 2, keepdims=False).reshape(tok, inner)
    came = send(leave, [(a, a, 1) for a in used])
    pair = jnp.where(
        side == 0, jnp.concatenate([stay, came], axis=0), jnp.concatenate([came, stay], axis=0)
    )
    piles = [pair] + [send(pair, [(a, a, 2 * k) for a in used]) for k in range(1, half)]
    states = jnp.concatenate(piles, axis=0)
    fresh_states = [send(states, [(sections - TICKS + 1 + i, 0, 0)]) for i in range(TICKS - 1)]
    block = layer(
        states, mine_first, theirs_first, place, [(a, a, 1) for a in range(last_full + 1)]
    )
    block = token_order(block)
    for tick in range(1, TICKS):
        top = last_full + tick
        piles = [send(block, [(a - 1, a, 2 * k) for a in range(1, top + 1)]) for k in range(half)]
        states = jnp.where(section == 0, fresh_states[tick - 1], jnp.concatenate(piles, axis=1))
        block = layer(
            states, mine_late, theirs_late, place - flips, [(a, a, 1) for a in range(top + 1)]
        )
        block = jnp.where(section == 0, token_order(block), block)
    tokens = lax.all_to_all(block, "dp", split_axis=0, concat_axis=1, tiled=True)
    shifted = send(tokens, [(a, a + 1, 0) for a in range(sections - 1)])
    held_out = jnp.where(section == 0, fresh_batches[TICKS - 1], shifted)

    def spread(x):
        return lax.all_to_all(
            jnp.broadcast_to(x[None], (dps, *x.shape)), "dp", split_axis=0, concat_axis=0
        )

    every = SEQ // tok
    ends = spread(held_states[0, tok - 1 :])[every - 1 :: every, 0]
    exits = []
    for tick in range(TICKS):
        wide = ends.astype(jnp.float32)
        inv_rms = lax.rsqrt(jnp.mean(wide * wide, axis=-1, keepdims=True) + epsilon)
        normed = (wide * inv_rms * gain).astype(jnp.bfloat16)
        projected = jnp.dot(normed, weight, preferred_element_type=jnp.float32).astype(jnp.bfloat16)
        kept = lax.dynamic_slice_in_dim(wide, dp * cols, cols, axis=1)
        piece = (kept + jax.nn.silu(projected.astype(jnp.float32))).astype(jnp.bfloat16)
        exits.append(piece)
        if tick < TICKS - 1:
            piece = send(piece, [(a, a + 1, 0) for a in range(sections - 1)])
            ends = jnp.concatenate(list(spread(piece)), axis=1)
    passages = ends.shape[0]
    exit_pieces = lax.all_gather(jnp.concatenate(exits, axis=0), "section", axis=0)[sections - 1]
    exit_rows = jnp.concatenate(list(spread(exit_pieces)), axis=1)
    scaled = exit_rows.astype(jnp.float32) * final_gain
    embedded = (
        scaled * lax.rsqrt(jnp.sum(scaled * scaled, axis=-1, keepdims=True) + epsilon)
    ).astype(jnp.bfloat16)
    per_peer = rows // dps
    source = jnp.arange(rows) // per_peer
    passage = source // every
    is_end = source % every == every - 1
    slot = inbox[:, width].astype(jnp.int32)
    replaced = is_end & (slot < TICKS)
    pick = jnp.where(replaced, slot * passages + passage, -1)
    chosen = (pick[:, None] == jnp.arange(TICKS * passages)).astype(jnp.bfloat16)
    received = jnp.where(
        replaced[:, None],
        jnp.dot(chosen, embedded, preferred_element_type=jnp.float32).astype(jnp.bfloat16),
        inbox[:, :width],
    )
    all_scores = lax.dot_general(
        queries, received, (((1,), (1,)), ((), ())), preferred_element_type=jnp.float32
    )
    listed = shortlist[..., None] == jnp.arange(rows, dtype=jnp.int32)
    student = jnp.sum(jnp.where(listed, all_scores[:, None, :], 0.0), axis=-1) * logit_scale
    student_log = jax.nn.log_softmax(student, axis=-1)
    teacher_log = jax.nn.log_softmax(teacher, axis=-1)
    teacher_prob = jnp.exp(teacher_log)
    losses = jnp.sum(teacher_prob * (teacher_log - student_log), axis=-1)
    logit_grad = logit_scale * (jnp.exp(student_log) - teacher_prob)
    row_grad = jnp.sum(jnp.where(listed, logit_grad[..., None], 0.0), axis=1)
    received_wide = received.astype(jnp.float32)
    owner_grads = lax.all_gather(row_grad, "section", axis=0, tiled=True)
    received_grad = jnp.dot(
        owner_grads.T, owner_queries.astype(jnp.float32), precision=lax.Precision.HIGHEST
    ).astype(jnp.bfloat16)
    query_grad = jnp.dot(row_grad, received_wide, precision=lax.Precision.HIGHEST)
    returned = lax.all_to_all(received_grad, "dp", split_axis=0, concat_axis=0, tiled=True)
    pool_grad = jnp.zeros(returned.shape, jnp.bfloat16).at[route[0]].set(returned)
    return (held_out[None], losses, query_grad, pool_grad)


def solution(mesh):
    return jax.shard_map(
        on_device,
        mesh=mesh,
        in_specs=(
            P(None, "dp", None),
            P("section", "dp", None),
            P("section", None, "dp"),
            P("section", None),
            P(),
            P("dp", None),
            P("dp", None),
            P(("section", "dp"), None),
            P(("section", "dp"), None),
            P(("section", "dp"), None),
        ),
        out_specs=(
            P("section", "dp", None),
            P(("section", "dp")),
            P(("section", "dp"), None),
            P("dp", None),
        ),
        check_vma=False,
    )
```

profile of v0, /device:TPU:0, one launch (start us, length us, event | category | flops | bytes accessed | tf_op | source)
XLA Modules:
  0.0 322.5 jit_solution(15851997710125030554)
XLA Ops:
  3.9 7.3 %all-to-all-start.2 = ((bf16[8,2,2048]{2,1,0:T(2,128)(2,1)}), bf16[8,2,2048]{2,1,0:T(2,128)(2,1)S(1)}, u32[]{:S(2)}, u32[]{:S(2)}) async-start(bf16[8,2,2048]{2,1,0:T(2,128)(2,1)} %reshape.406), calls=%async_computation.2 | async-start | bytes 131072 | tf_op jit(solution)/shard_map/all_to_all | solution.py:122
  17.5 3.9 %collective-permute-start.6 = (bf16[4,512,512]{2,1,0:T(8,128)(2,1)}, bf16[4,512,512]{2,1,0:T(8,128)(2,1)}, u32[]{:S(2)}, u32[]{:S(2)}) collective-permute-start(bf16[4,512,512]{2,1,0:T(8,128)(2,1)} %get-tuple-element.18), channel_id=1, source_target_pairs={{0,1},{1,0},{2,3},{3,2},{4,5},{5,4},{6,7},{7,6},{8,9},{9,8},{10,11... | collective-permute-start | bytes 6291464 | tf_op jit(solution)/shard_map/ppermute | solution.py:38
  41.3 6.0 %all-to-all-start.3 = ((bf16[8,4,512]{2,1,0:T(4,128)(2,1)}), bf16[8,4,512]{2,1,0:T(4,128)(2,1)S(1)}, u32[]{:S(2)}, u32[]{:S(2)}) async-start(bf16[8,4,512]{2,1,0:T(4,128)(2,1)} %broadcast_in_dim.126), calls=%async_computation.3 | async-start | bytes 65536 | tf_op jit(solution)/shard_map/all_to_all | solution.py:122
  47.3 22.6 %all-to-all-done.3 = bf16[8,4,512]{2,1,0:T(4,128)(2,1)S(1)} async-done(((bf16[8,4,512]{2,1,0:T(4,128)(2,1)}), bf16[8,4,512]{2,1,0:T(4,128)(2,1)S(1)}, u32[]{:S(2)}, u32[]{:S(2)}) %all-to-all-start.3) | async-done | bytes 32800 | tf_op jit(solution)/shard_map/all_to_all | solution.py:122
  77.7 5.7 %all-to-all-start.4 = ((bf16[8,4,512]{2,1,0:T(4,128)(2,1)}), bf16[8,4,512]{2,1,0:T(4,128)(2,1)S(1)}, u32[]{:S(2)}, u32[]{:S(2)}) async-start(bf16[8,4,512]{2,1,0:T(4,128)(2,1)} %broadcast_in_dim.127), calls=%async_computation.4 | async-start | bytes 65536 | tf_op jit(solution)/shard_map/all_to_all | solution.py:122
  83.4 5.8 %all_gather.15 = bf16[32,4096]{1,0:T(8,128)(2,1)S(1)} all-gather(bf16[8,4096]{1,0:T(8,128)(2,1)S(1)} %copy-done.10), channel_id=1, replica_groups=mesh['section'=4,'dp'=8] {'section'}, dimensions={0}, use_global_device_ids=true | all-gather | bytes 327680 | tf_op jit(solution)/shard_map/all_gather | solution.py:53
  94.6 4.3 %collective-permute-start.2 = (bf16[128,2048]{1,0:T(8,128)(2,1)S(1)}, bf16[128,2048]{1,0:T(8,128)(2,1)S(1)}, u32[]{:S(2)}, u32[]{:S(2)}) collective-permute-start(bf16[128,2048]{1,0:T(8,128)(2,1)S(1)} %maximum_select_fusion.2), channel_id=1, source_target_pairs={{0,4},{1,5},{2,6},{3,7},{4,0},{5,1},{6,2},{7,3},{16,20},{17,21},{1... | collective-permute-start | bytes 1572872 | tf_op jit(solution)/shard_map/ppermute | solution.py:38
  104.6 5.2 %all-gather.1 = bf16[4,12,512]{2,1,0:T(8,128)(2,1)S(1)} all-gather(bf16[1,12,512]{2,1,0:T(8,128)(2,1)S(1)} %maximum_bitcast_fusion), channel_id=2, replica_groups=mesh['section'=4,'dp'=8] {'section'}, dimensions={0}, use_global_device_ids=true | all-gather | bytes 61440 | tf_op jit(solution)/shard_map/all_gather | solution.py:141
  110.5 5.1 %all-to-all-start.5 = ((bf16[8,12,512]{2,1,0:T(8,128)(2,1)}), bf16[8,12,512]{2,1,0:T(8,128)(2,1)S(1)}, u32[]{:S(2)}, u32[]{:S(2)}) async-start(bf16[8,12,512]{2,1,0:T(8,128)(2,1)} %broadcast_in_dim.129), calls=%async_computation.5 | async-start | bytes 262144 | tf_op jit(solution)/shard_map/all_to_all | solution.py:122
  121.0 3.6 %gather_fusion.2 = bf16[4,512,512]{2,1,0:T(8,128)(2,1)} fusion(bf16[4,512,512]{2,1,0:T(8,128)(2,1)} %collective-permute-done.6, s32[1024]{0:T(1024)S(1)} %pad_clamp_fusion.2), kind=kCustom, calls=%fused_computation.2.clone | custom fusion | bytes 4194320 | tf_op jit(solution)/shard_map/jit(_take)/gather | solution.py:65
  124.6 3.4 %broadcast_select_fusion.1 = (bf16[4,512,512]{2,1,0:T(8,128)(2,1)}, bf16[4,512,512]{2,1,0:T(8,128)(2,1)S(1)}) fusion(bf16[4,512,512]{2,1,0:T(8,128)(2,1)S(1)} %copy-done.1, pred[4]{0:T(512)(128)(4,1)S(1)} %compare_and_fusion.2, bf16[4,512,512]{2,1,0:T(8,128)(2,1)} %gather_fusion.2), kind=kLoop, calls=%fused_computation.28 | loop fusion | flops 2097152 | bytes 8388612 | tf_op jit(solution)/shard_map/jit(_take)/select_n | solution.py:65
  128.0 4.5 %convolution_convert_fusion.4 = bf16[512,512]{1,0:T(8,128)(2,1)} fusion(bf16[512,2048]{1,0:T(8,128)(2,1)} %get-tuple-element.16, bf16[2048,512]{1,0:T(8,128)(2,1)S(1)} %bitcast.209), kind=kOutput, calls=%fused_computation.46 | convolution fusion | flops 1074003968 | bytes 4718592 | tf_op jit(solution)/shard_map/dot_general | solution.py:79
  132.4 3.4 %collective-permute-start.7 = (bf16[512,512]{1,0:T(8,128)(2,1)}, bf16[512,512]{1,0:T(8,128)(2,1)}, u32[]{:S(2)}, u32[]{:S(2)}) collective-permute-start(bf16[512,512]{1,0:T(8,128)(2,1)} %convolution_convert_fusion.4), channel_id=1, source_target_pairs={{0,1},{1,0},{2,3},{3,2},{4,5},{5,4},{6,7},{7,6}} | collective-permute-start | bytes 1572872 | tf_op jit(solution)/shard_map/ppermute | solution.py:38
  135.8 10.5 %all-to-all-start.1 = ((bf16[8,8,4224]{2,1,0:T(8,128)(2,1)}), bf16[8,8,4224]{2,1,0:T(8,128)(2,1)}, u32[]{:S(2)}, u32[]{:S(2)}) async-start(bf16[8,8,4224]{2,1,0:T(8,128)(2,1)} %pad_maximum_fusion.1), calls=%async_computation.1 | async-start | bytes 1081344 | tf_op jit(solution)/shard_map/all_to_all | solution.py:52
  146.9 3.9 %collective-permute-start.8 = (f32[512]{0:T(512)S(1)}, f32[512]{0:T(512)S(1)}, u32[]{:S(2)}, u32[]{:S(2)}) collective-permute-start(f32[512]{0:T(512)S(1)} %get-tuple-element.15), channel_id=1, source_target_pairs={{0,1},{1,0},{2,3},{3,2},{4,5},{5,4},{6,7},{7,6}} | collective-permute-start | bytes 6152 | tf_op jit(solution)/shard_map/ppermute | solution.py:38
  152.6 3.3 %add_convert_fusion.2 = bf16[512,512]{1,0:T(8,128)(2,1)S(1)} fusion(bf16[512,512]{1,0:T(8,128)(2,1)} %collective-permute-done.7, bf16[512,2048]{1,0:T(8,128)(2,1)} %get-tuple-element.16, bf16[2048,512]{1,0:T(8,128)(2,1)S(1)} %bitcast.207, f32[512]{0:T(512)S(1)} %add_rsqrt_fusion.2, s32[]{:T(128)S(6)} %select_n.203), kind=kOutput, calls=%fused_computation.65 | convolution fusion | flops 1076887552 | bytes 5769220 | tf_op jit(solution)/shard_map/dot_general | solution.py:81
  165.3 5.0 %collective-permute-done.11 = bf16[512,512]{1,0:T(8,128)(2,1)S(1)} collective-permute-done((bf16[512,512]{1,0:T(8,128)(2,1)S(1)}, bf16[512,512]{1,0:T(8,128)(2,1)S(1)}, u32[]{:S(2)}, u32[]{:S(2)}) %collective-permute-start.11) | collective-permute-done | bytes 524320 | tf_op jit(solution)/shard_map/ppermute | solution.py:38
  170.3 5.6 %collective-permute-done.12 = bf16[512,512]{1,0:T(8,128)(2,1)S(1)} collective-permute-done((bf16[512,512]{1,0:T(8,128)(2,1)S(1)}, bf16[512,512]{1,0:T(8,128)(2,1)S(1)}, u32[]{:S(2)}, u32[]{:S(2)}) %collective-permute-start.12) | collective-permute-done | bytes 524320 | tf_op jit(solution)/shard_map/ppermute | solution.py:38
  179.5 3.9 %collective-permute-start.13 = (bf16[512,512]{1,0:T(8,128)(2,1)S(1)}, bf16[512,512]{1,0:T(8,128)(2,1)S(1)}, u32[]{:S(2)}, u32[]{:S(2)}) collective-permute-start(bf16[512,512]{1,0:T(8,128)(2,1)S(1)} %convolution_convert_fusion.3), channel_id=1, source_target_pairs={{0,1},{1,0},{2,3},{3,2},{4,5},{5,4},{6,7},{7,6},{8,9},{9,8},{10,11... | collective-permute-start | bytes 1572872 | tf_op jit(solution)/shard_map/ppermute | solution.py:38
  186.6 7.2 %collective-permute-done.14 = f32[512]{0:T(512)S(1)} collective-permute-done((f32[512]{0:T(512)S(1)}, f32[512]{0:T(512)S(1)}, u32[]{:S(2)}, u32[]{:S(2)}) %collective-permute-start.14) | collective-permute-done | bytes 2080 | tf_op jit(solution)/shard_map/ppermute | solution.py:38
  197.9 4.5 %collective-permute-start.15 = (bf16[512,512]{1,0:T(8,128)(2,1)S(1)}, bf16[512,512]{1,0:T(8,128)(2,1)S(1)}, u32[]{:S(2)}, u32[]{:S(2)}) collective-permute-start(bf16[512,512]{1,0:T(8,128)(2,1)S(1)} %bitcast_select_fusion.2), channel_id=1, source_target_pairs={{0,8},{1,9},{2,10},{3,11},{4,12},{5,13},{6,14},{7,15},{8,16},{9,17... | collective-permute-start | bytes 1572872 | tf_op jit(solution)/shard_map/ppermute | solution.py:38
  202.5 10.1 %collective-permute-start.16 = (bf16[512,512]{1,0:T(8,128)(2,1)S(1)}, bf16[512,512]{1,0:T(8,128)(2,1)S(1)}, u32[]{:S(2)}, u32[]{:S(2)}) collective-permute-start(bf16[512,512]{1,0:T(8,128)(2,1)S(1)} %bitcast_select_fusion.2), channel_id=1, source_target_pairs={{0,10},{1,11},{2,8},{3,9},{4,14},{5,15},{6,12},{7,13},{8,18},{9,19... | collective-permute-start | bytes 1572872 | tf_op jit(solution)/shard_map/ppermute | solution.py:38
  215.5 9.4 %collective-permute-done.16 = bf16[512,512]{1,0:T(8,128)(2,1)S(1)} collective-permute-done((bf16[512,512]{1,0:T(8,128)(2,1)S(1)}, bf16[512,512]{1,0:T(8,128)(2,1)S(1)}, u32[]{:S(2)}, u32[]{:S(2)}) %collective-permute-start.16) | collective-permute-done | bytes 524320 | tf_op jit(solution)/shard_map/ppermute | solution.py:38
  224.9 8.7 %collective-permute-done.17 = bf16[512,512]{1,0:T(8,128)(2,1)S(1)} collective-permute-done((bf16[512,512]{1,0:T(8,128)(2,1)S(1)}, bf16[512,512]{1,0:T(8,128)(2,1)S(1)}, u32[]{:S(2)}, u32[]{:S(2)}) %collective-permute-start.17) | collective-permute-done | bytes 524320 | tf_op jit(solution)/shard_map/ppermute | solution.py:38
  233.6 5.6 %collective-permute-done.18 = bf16[512,512]{1,0:T(8,128)(2,1)S(1)} collective-permute-done((bf16[512,512]{1,0:T(8,128)(2,1)S(1)}, bf16[512,512]{1,0:T(8,128)(2,1)S(1)}, u32[]{:S(2)}, u32[]{:S(2)}) %collective-permute-start.18) | collective-permute-done | bytes 524320 | tf_op jit(solution)/shard_map/ppermute | solution.py:38
  241.6 3.6 %collective-permute-start.19 = (bf16[512,512]{1,0:T(8,128)(2,1)S(1)}, bf16[512,512]{1,0:T(8,128)(2,1)S(1)}, u32[]{:S(2)}, u32[]{:S(2)}) collective-permute-start(bf16[512,512]{1,0:T(8,128)(2,1)S(1)} %convolution_convert_fusion.2), channel_id=1, source_target_pairs={{0,1},{1,0},{2,3},{3,2},{4,5},{5,4},{6,7},{7,6},{8,9},{9,8},{10,11... | collective-permute-start | bytes 1572872 | tf_op jit(solution)/shard_map/ppermute | solution.py:38
  252.7 3.9 %add_convert_fusion = bf16[512,512]{1,0:T(8,128)(2,1)S(1)} fusion(f32[512]{0:T(512)S(1)} %add_rsqrt_fusion, bf16[512,512]{1,0:T(8,128)(2,1)S(1)} %collective-permute-done.19, bf16[512,2048]{1,0:T(8,128)(2,1)} %copy-done.2, bf16[2048,512]{1,0:T(8,128)(2,1)} %bitcast.206, s32[]{:T(128)S(6)} %select_n.206), kind=kOutput, calls=%fused_computation.63 | convolution fusion | flops 1076887552 | bytes 5769220 | tf_op jit(solution)/shard_map/dot_general | solution.py:81
  258.2 27.3 %all-to-all-start = ((bf16[8,64,512]{2,1,0:T(8,128)(2,1)}), bf16[8,64,512]{2,1,0:T(8,128)(2,1)S(1)}, u32[]{:S(2)}, u32[]{:S(2)}) async-start(bf16[8,64,512]{2,1,0:T(8,128)(2,1)} %bitcast.12), calls=%async_computation | async-start | bytes 1048576 | tf_op jit(solution)/shard_map/all_to_all | solution.py:117
  287.0 5.2 %all_gather.14 = f32[32,64]{1,0:T(8,128)S(1)} all-gather(f32[8,64]{1,0:T(8,128)S(1)} %select_reduce_fusion), channel_id=1, replica_groups=mesh['section'=4,'dp'=8] {'section'}, dimensions={0}, use_global_device_ids=true | all-gather | bytes 10240 | tf_op jit(solution)/shard_map/all_gather | solution.py:172
  293.6 6.4 %all-to-all-done = bf16[8,64,512]{2,1,0:T(8,128)(2,1)S(1)} async-done(((bf16[8,64,512]{2,1,0:T(8,128)(2,1)}), bf16[8,64,512]{2,1,0:T(8,128)(2,1)S(1)}, u32[]{:S(2)}, u32[]{:S(2)}) %all-to-all-start) | async-done | bytes 524320 | tf_op jit(solution)/shard_map/all_to_all | solution.py:117
  300.1 3.6 %all-to-all-start.6 = ((bf16[8,8,4096]{2,1,0:T(8,128)(2,1)}), bf16[8,8,4096]{2,1,0:T(8,128)(2,1)S(1)}, u32[]{:S(2)}, u32[]{:S(2)}) async-start(bf16[8,8,4096]{2,1,0:T(8,128)(2,1)} %fusion.2), calls=%async_computation.6 | async-start | bytes 1048576 | tf_op jit(solution)/shard_map/all_to_all | solution.py:177
  306.4 12.0 %all-to-all-done.6 = bf16[8,8,4096]{2,1,0:T(8,128)(2,1)S(1)} async-done(((bf16[8,8,4096]{2,1,0:T(8,128)(2,1)}), bf16[8,8,4096]{2,1,0:T(8,128)(2,1)S(1)}, u32[]{:S(2)}, u32[]{:S(2)}) %all-to-all-start.6) | async-done | bytes 524320 | tf_op jit(solution)/shard_map/all_to_all | solution.py:177
  (202 shorter events, 100.5 us)
Async XLA Ops:
  0.6 32.3 %copy-start = (bf16[64,4096]{1,0:T(8,128)(2,1)S(1)}, bf16[64,4096]{1,0:T(8,128)(2,1)}, u32[]{:S(2)}) copy-start(bf16[64,4096]{1,0:T(8,128)(2,1)} %param.20) | copy-start | bytes 1572868
  3.9 31.4 %all-to-all-start.2 = ((bf16[8,2,2048]{2,1,0:T(2,128)(2,1)}), bf16[8,2,2048]{2,1,0:T(2,128)(2,1)S(1)}, u32[]{:S(2)}, u32[]{:S(2)}) async-start(bf16[8,2,2048]{2,1,0:T(2,128)(2,1)} %reshape.406), calls=%async_computation.2 | async-start | bytes 131072 | tf_op jit(solution)/shard_map/all_to_all | solution.py:122
  17.5 103.5 %collective-permute-start.6 = (bf16[4,512,512]{2,1,0:T(8,128)(2,1)}, bf16[4,512,512]{2,1,0:T(8,128)(2,1)}, u32[]{:S(2)}, u32[]{:S(2)}) collective-permute-start(bf16[4,512,512]{2,1,0:T(8,128)(2,1)} %get-tuple-element.18), channel_id=1, source_target_pairs={{0,1},{1,0},{2,3},{3,2},{4,5},{5,4},{6,7},{7,6},{8,9},{9,8},{10,11... | collective-permute-start | bytes 6291464 | tf_op jit(solution)/shard_map/ppermute | solution.py:38
  29.0 61.4 %collective-permute-start = (bf16[64,2048]{1,0:T(8,128)(2,1)}, bf16[64,2048]{1,0:T(8,128)(2,1)}, u32[]{:S(2)}, u32[]{:S(2)}) collective-permute-start(bf16[64,2048]{1,0:T(8,128)(2,1)} %bitcast.57), channel_id=1, source_target_pairs={{0,1},{1,0},{2,3},{3,2},{4,5},{5,4},{6,7},{7,6},{16,17},{17,16},{1... | collective-permute-start | bytes 786440 | tf_op jit(solution)/shard_map/ppermute | solution.py:38
  38.6 2.1 collective-permute-start.22
  41.3 28.6 %all-to-all-start.3 = ((bf16[8,4,512]{2,1,0:T(4,128)(2,1)}), bf16[8,4,512]{2,1,0:T(4,128)(2,1)S(1)}, u32[]{:S(2)}, u32[]{:S(2)}) async-start(bf16[8,4,512]{2,1,0:T(4,128)(2,1)} %broadcast_in_dim.126), calls=%async_computation.3 | async-start | bytes 65536 | tf_op jit(solution)/shard_map/all_to_all | solution.py:122
  73.1 4.0 %collective-permute-start.23 = (bf16[4,512]{1,0:T(4,128)(2,1)S(1)}, bf16[4,512]{1,0:T(4,128)(2,1)S(1)}, u32[]{:S(2)}, u32[]{:S(2)}) collective-permute-start(bf16[4,512]{1,0:T(4,128)(2,1)S(1)} %fusion.81), channel_id=1, source_target_pairs={{0,8},{1,9},{2,10},{3,11},{4,12},{5,13},{6,14},{7,15},{8,16},{9,17... | collective-permute-start | bytes 12296 | tf_op jit(solution)/shard_map/ppermute | solution.py:38
  77.7 12.4 %all-to-all-start.4 = ((bf16[8,4,512]{2,1,0:T(4,128)(2,1)}), bf16[8,4,512]{2,1,0:T(4,128)(2,1)S(1)}, u32[]{:S(2)}, u32[]{:S(2)}) async-start(bf16[8,4,512]{2,1,0:T(4,128)(2,1)} %broadcast_in_dim.127), calls=%async_computation.4 | async-start | bytes 65536 | tf_op jit(solution)/shard_map/all_to_all | solution.py:122
  91.5 24.1 %collective-permute-start.1 = (bf16[128,2048]{1,0:T(8,128)(2,1)S(1)}, bf16[128,2048]{1,0:T(8,128)(2,1)S(1)}, u32[]{:S(2)}, u32[]{:S(2)}) collective-permute-start(bf16[128,2048]{1,0:T(8,128)(2,1)S(1)} %maximum_select_fusion.2), channel_id=1, source_target_pairs={{0,2},{1,3},{2,0},{3,1},{4,6},{5,7},{6,4},{7,5},{16,18},{17,19},{1... | collective-permute-start | bytes 1572872 | tf_op jit(solution)/shard_map/ppermute | solution.py:38
  94.6 23.3 %collective-permute-start.2 = (bf16[128,2048]{1,0:T(8,128)(2,1)S(1)}, bf16[128,2048]{1,0:T(8,128)(2,1)S(1)}, u32[]{:S(2)}, u32[]{:S(2)}) collective-permute-start(bf16[128,2048]{1,0:T(8,128)(2,1)S(1)} %maximum_select_fusion.2), channel_id=1, source_target_pairs={{0,4},{1,5},{2,6},{3,7},{4,0},{5,1},{6,2},{7,3},{16,20},{17,21},{1... | collective-permute-start | bytes 1572872 | tf_op jit(solution)/shard_map/ppermute | solution.py:38
  98.8 19.0 %collective-permute-start.3 = (bf16[128,2048]{1,0:T(8,128)(2,1)S(1)}, bf16[128,2048]{1,0:T(8,128)(2,1)S(1)}, u32[]{:S(2)}, u32[]{:S(2)}) collective-permute-start(bf16[128,2048]{1,0:T(8,128)(2,1)S(1)} %maximum_select_fusion.2), channel_id=1, source_target_pairs={{0,6},{1,7},{2,4},{3,5},{4,2},{5,3},{6,0},{7,1},{16,22},{17,23},{1... | collective-permute-start | bytes 1572872 | tf_op jit(solution)/shard_map/ppermute | solution.py:38
  110.5 25.3 %all-to-all-start.5 = ((bf16[8,12,512]{2,1,0:T(8,128)(2,1)}), bf16[8,12,512]{2,1,0:T(8,128)(2,1)S(1)}, u32[]{:S(2)}, u32[]{:S(2)}) async-start(bf16[8,12,512]{2,1,0:T(8,128)(2,1)} %broadcast_in_dim.129), calls=%async_computation.5 | async-start | bytes 262144 | tf_op jit(solution)/shard_map/all_to_all | solution.py:122
  119.4 44.5 %collective-permute-start.5 = (bf16[512,2048]{1,0:T(8,128)(2,1)}, bf16[512,2048]{1,0:T(8,128)(2,1)}, u32[]{:S(2)}, u32[]{:S(2)}) collective-permute-start(bf16[512,2048]{1,0:T(8,128)(2,1)} %get-tuple-element.16), channel_id=1, source_target_pairs={{16,0},{17,1},{18,2},{19,3},{20,4},{21,5},{22,6},{23,7}} | collective-permute-start | bytes 6291464 | tf_op jit(solution)/shard_map/ppermute | solution.py:38
  132.4 20.1 %collective-permute-start.7 = (bf16[512,512]{1,0:T(8,128)(2,1)}, bf16[512,512]{1,0:T(8,128)(2,1)}, u32[]{:S(2)}, u32[]{:S(2)}) collective-permute-start(bf16[512,512]{1,0:T(8,128)(2,1)} %convolution_convert_fusion.4), channel_id=1, source_target_pairs={{0,1},{1,0},{2,3},{3,2},{4,5},{5,4},{6,7},{7,6}} | collective-permute-start | bytes 1572872 | tf_op jit(solution)/shard_map/ppermute | solution.py:38
  135.8 109.3 %all-to-all-start.1 = ((bf16[8,8,4224]{2,1,0:T(8,128)(2,1)}), bf16[8,8,4224]{2,1,0:T(8,128)(2,1)}, u32[]{:S(2)}, u32[]{:S(2)}) async-start(bf16[8,8,4224]{2,1,0:T(8,128)(2,1)} %pad_maximum_fusion.1), calls=%async_computation.1 | async-start | bytes 1081344 | tf_op jit(solution)/shard_map/all_to_all | solution.py:52
  146.9 5.7 %collective-permute-start.8 = (f32[512]{0:T(512)S(1)}, f32[512]{0:T(512)S(1)}, u32[]{:S(2)}, u32[]{:S(2)}) collective-permute-start(f32[512]{0:T(512)S(1)} %get-tuple-element.15), channel_id=1, source_target_pairs={{0,1},{1,0},{2,3},{3,2},{4,5},{5,4},{6,7},{7,6}} | collective-permute-start | bytes 6152 | tf_op jit(solution)/shard_map/ppermute | solution.py:38
  156.6 8.6 %collective-permute-start.10 = (bf16[512,512]{1,0:T(8,128)(2,1)S(1)}, bf16[512,512]{1,0:T(8,128)(2,1)S(1)}, u32[]{:S(2)}, u32[]{:S(2)}) collective-permute-start(bf16[512,512]{1,0:T(8,128)(2,1)S(1)} %bitcast.216), channel_id=1, source_target_pairs={{0,10},{1,11},{2,8},{3,9},{4,14},{5,15},{6,12},{7,13}} | collective-permute-start | bytes 1572872 | tf_op jit(solution)/shard_map/ppermute | solution.py:38
  158.0 12.3 %collective-permute-start.11 = (bf16[512,512]{1,0:T(8,128)(2,1)S(1)}, bf16[512,512]{1,0:T(8,128)(2,1)S(1)}, u32[]{:S(2)}, u32[]{:S(2)}) collective-permute-start(bf16[512,512]{1,0:T(8,128)(2,1)S(1)} %bitcast.217), channel_id=1, source_target_pairs={{0,12},{1,13},{2,14},{3,15},{4,8},{5,9},{6,10},{7,11}} | collective-permute-start | bytes 1572872 | tf_op jit(solution)/shard_map/ppermute | solution.py:38
  159.3 16.6 %collective-permute-start.12 = (bf16[512,512]{1,0:T(8,128)(2,1)S(1)}, bf16[512,512]{1,0:T(8,128)(2,1)S(1)}, u32[]{:S(2)}, u32[]{:S(2)}) collective-permute-start(bf16[512,512]{1,0:T(8,128)(2,1)S(1)} %bitcast.218), channel_id=1, source_target_pairs={{0,14},{1,15},{2,12},{3,13},{4,10},{5,11},{6,8},{7,9}} | collective-permute-start | bytes 1572872 | tf_op jit(solution)/shard_map/ppermute | solution.py:38
  160.6 15.3 %collective-permute-start.9 = (bf16[512,512]{1,0:T(8,128)(2,1)S(1)}, bf16[512,512]{1,0:T(8,128)(2,1)S(1)}, u32[]{:S(2)}, u32[]{:S(2)}) collective-permute-start(bf16[512,512]{1,0:T(8,128)(2,1)S(1)} %bitcast.219), channel_id=1, source_target_pairs={{0,8},{1,9},{2,10},{3,11},{4,12},{5,13},{6,14},{7,15}} | collective-permute-start | bytes 1572872 | tf_op jit(solution)/shard_map/ppermute | solution.py:38
  163.9 51.6 %collective-permute-start.4 = (bf16[512,2048]{1,0:T(8,128)(2,1)}, bf16[512,2048]{1,0:T(8,128)(2,1)S(1)}, u32[]{:S(2)}, u32[]{:S(2)}) collective-permute-start(bf16[512,2048]{1,0:T(8,128)(2,1)} %get-tuple-element.16), channel_id=1, source_target_pairs={{24,0},{25,1},{26,2},{27,3},{28,4},{29,5},{30,6},{31,7}} | collective-permute-start | bytes 6291464 | tf_op jit(solution)/shard_map/ppermute | solution.py:38
  179.5 14.3 %collective-permute-start.13 = (bf16[512,512]{1,0:T(8,128)(2,1)S(1)}, bf16[512,512]{1,0:T(8,128)(2,1)S(1)}, u32[]{:S(2)}, u32[]{:S(2)}) collective-permute-start(bf16[512,512]{1,0:T(8,128)(2,1)S(1)} %convolution_convert_fusion.3), channel_id=1, source_target_pairs={{0,1},{1,0},{2,3},{3,2},{4,5},{5,4},{6,7},{7,6},{8,9},{9,8},{10,11... | collective-permute-start | bytes 1572872 | tf_op jit(solution)/shard_map/ppermute | solution.py:38
  184.0 9.7 %collective-permute-start.14 = (f32[512]{0:T(512)S(1)}, f32[512]{0:T(512)S(1)}, u32[]{:S(2)}, u32[]{:S(2)}) collective-permute-start(f32[512]{0:T(512)S(1)} %get-tuple-element.13), channel_id=1, source_target_pairs={{0,1},{1,0},{2,3},{3,2},{4,5},{5,4},{6,7},{7,6},{8,9},{9,8},{10,11... | collective-permute-start | bytes 6152 | tf_op jit(solution)/shard_map/ppermute | solution.py:38
  197.9 17.5 %collective-permute-start.15 = (bf16[512,512]{1,0:T(8,128)(2,1)S(1)}, bf16[512,512]{1,0:T(8,128)(2,1)S(1)}, u32[]{:S(2)}, u32[]{:S(2)}) collective-permute-start(bf16[512,512]{1,0:T(8,128)(2,1)S(1)} %bitcast_select_fusion.2), channel_id=1, source_target_pairs={{0,8},{1,9},{2,10},{3,11},{4,12},{5,13},{6,14},{7,15},{8,16},{9,17... | collective-permute-start | bytes 1572872 | tf_op jit(solution)/shard_map/ppermute | solution.py:38
  202.5 22.4 %collective-permute-start.16 = (bf16[512,512]{1,0:T(8,128)(2,1)S(1)}, bf16[512,512]{1,0:T(8,128)(2,1)S(1)}, u32[]{:S(2)}, u32[]{:S(2)}) collective-permute-start(bf16[512,512]{1,0:T(8,128)(2,1)S(1)} %bitcast_select_fusion.2), channel_id=1, source_target_pairs={{0,10},{1,11},{2,8},{3,9},{4,14},{5,15},{6,12},{7,13},{8,18},{9,19... | collective-permute-start | bytes 1572872 | tf_op jit(solution)/shard_map/ppermute | solution.py:38
  212.5 21.0 %collective-permute-start.17 = (bf16[512,512]{1,0:T(8,128)(2,1)S(1)}, bf16[512,512]{1,0:T(8,128)(2,1)S(1)}, u32[]{:S(2)}, u32[]{:S(2)}) collective-permute-start(bf16[512,512]{1,0:T(8,128)(2,1)S(1)} %bitcast_select_fusion.2), channel_id=1, source_target_pairs={{0,12},{1,13},{2,14},{3,15},{4,8},{5,9},{6,10},{7,11},{8,20},{9,21... | collective-permute-start | bytes 1572872 | tf_op jit(solution)/shard_map/ppermute | solution.py:38
  213.9 25.3 %collective-permute-start.18 = (bf16[512,512]{1,0:T(8,128)(2,1)S(1)}, bf16[512,512]{1,0:T(8,128)(2,1)S(1)}, u32[]{:S(2)}, u32[]{:S(2)}) collective-permute-start(bf16[512,512]{1,0:T(8,128)(2,1)S(1)} %bitcast_select_fusion.2), channel_id=1, source_target_pairs={{0,14},{1,15},{2,12},{3,13},{4,10},{5,11},{6,8},{7,9},{8,22},{9,23... | collective-permute-start | bytes 1572872 | tf_op jit(solution)/shard_map/ppermute | solution.py:38
  241.6 11.1 %collective-permute-start.19 = (bf16[512,512]{1,0:T(8,128)(2,1)S(1)}, bf16[512,512]{1,0:T(8,128)(2,1)S(1)}, u32[]{:S(2)}, u32[]{:S(2)}) collective-permute-start(bf16[512,512]{1,0:T(8,128)(2,1)S(1)} %convolution_convert_fusion.2), channel_id=1, source_target_pairs={{0,1},{1,0},{2,3},{3,2},{4,5},{5,4},{6,7},{7,6},{8,9},{9,8},{10,11... | collective-permute-start | bytes 1572872 | tf_op jit(solution)/shard_map/ppermute | solution.py:38
  246.1 6.5 %collective-permute-start.20 = (f32[512]{0:T(512)S(1)}, f32[512]{0:T(512)S(1)}, u32[]{:S(2)}, u32[]{:S(2)}) collective-permute-start(f32[512]{0:T(512)S(1)} %get-tuple-element.11), channel_id=1, source_target_pairs={{0,1},{1,0},{2,3},{3,2},{4,5},{5,4},{6,7},{7,6},{8,9},{9,8},{10,11... | collective-permute-start | bytes 6152 | tf_op jit(solution)/shard_map/ppermute | solution.py:38
  258.2 41.9 %all-to-all-start = ((bf16[8,64,512]{2,1,0:T(8,128)(2,1)}), bf16[8,64,512]{2,1,0:T(8,128)(2,1)S(1)}, u32[]{:S(2)}, u32[]{:S(2)}) async-start(bf16[8,64,512]{2,1,0:T(8,128)(2,1)} %bitcast.12), calls=%async_computation | async-start | bytes 1048576 | tf_op jit(solution)/shard_map/all_to_all | solution.py:117
  300.1 18.3 %all-to-all-start.6 = ((bf16[8,8,4096]{2,1,0:T(8,128)(2,1)}), bf16[8,8,4096]{2,1,0:T(8,128)(2,1)S(1)}, u32[]{:S(2)}, u32[]{:S(2)}) async-start(bf16[8,8,4096]{2,1,0:T(8,128)(2,1)} %fusion.2), calls=%async_computation.6 | async-start | bytes 1048576 | tf_op jit(solution)/shard_map/all_to_all | solution.py:177
  303.7 16.8 %collective-permute-start.21 = (bf16[64,4096]{1,0:T(8,128)(2,1)S(1)}, bf16[64,4096]{1,0:T(8,128)(2,1)S(1)}, u32[]{:S(2)}, u32[]{:S(2)}) collective-permute-start(bf16[64,4096]{1,0:T(8,128)(2,1)S(1)} %bitcast.215), channel_id=1, source_target_pairs={{0,8},{1,9},{2,10},{3,11},{4,12},{5,13},{6,14},{7,15},{8,16},{9,17... | collective-permute-start | bytes 1572872 | tf_op jit(solution)/shard_map/ppermute | solution.py:38
  (23 other events, 305.9 us)
where the time goes:
time: 324 us; the launch traced here: 322 us
  starting transfers between devices  130 us (40%)
  waiting for transfers between devices  90.5 us (28%)
  local copies, waits for them, and re-layouts  29.6 us (9%)
  matrix products  28.3 us (9%)
  other arithmetic  26.2 us (8%)
  blocking collectives  16.2 us (5%)
    ppermute x24, starting transfers between devices, send(): lax.ppermute(x, AXES, [(a * dps + i, b * dps + (i ^ flip)) for a, b, flip...  64.7 us
    ppermute x24, waiting for transfers between devices, send(): lax.ppermute(x, AXES, [(a * dps + i, b * dps + (i ^ flip)) for a, b, flip...  48.6 us
    all_to_all x1, starting transfers between devices, on_device(): lax.all_to_all(block, 'dp', split_axis=0, concat_axis=1, tiled=True)  27.3 us
    all_to_all x4, starting transfers between devices, spread(): lax.all_to_all(jnp.broadcast_to(x[None], (dps, *x.shape)), 'dp', split_ax...  24.1 us
    all_to_all x4, waiting for transfers between devices, spread(): lax.all_to_all(jnp.broadcast_to(x[None], (dps, *x.shape)), 'dp', split_ax...  23.5 us
    all_to_all x1, waiting for transfers between devices, on_device(): lax.all_to_all(received_grad, 'dp', split_axis=0, concat_axis=0, tiled=True)  12 us
    all_to_all x1, starting transfers between devices, on_device(): lax.all_to_all(outbox, 'dp', split_axis=0, concat_axis=0, tiled=True)  10.5 us
    dot_general x3, matrix products, layer(): own = jnp.dot(states, mine, preferred_element_type=jnp.float32)  8.69 us
  transfers between devices with their start and end apart: 31, of which 15 were waited for; matrix products, arithmetic and copies ran while one was open for 23% of the time, Pallas kernels for 0%

commit v1 on v0

--- a/solution.py
+++ b/solution.py
@@ -114,7 +114,19 @@
             states, mine_late, theirs_late, place - flips, [(a, a, 1) for a in range(top + 1)]
         )
         block = jnp.where(section == 0, token_order(block), block)
-    tokens = lax.all_to_all(block, "dp", split_axis=0, concat_axis=1, tiled=True)
+    ways, here = (lax.axis_size("dp"), lax.axis_index("dp"))
+    width_2 = block.shape[0] // ways
+    shape = list(block.shape)
+    shape[0] = width_2
+    height = shape[1]
+    shape[1] = height * ways
+    full = jnp.zeros(shape, block.dtype)
+    for mask in range(ways):
+        part = lax.dynamic_slice_in_dim(block, (here ^ mask) * width_2, width_2, axis=0)
+        if mask:
+            part = lax.ppermute(part, "dp", [(d, d ^ mask) for d in range(ways)])
+        full = lax.dynamic_update_slice_in_dim(full, part, (here ^ mask) * height, axis=1)
+    tokens = full
     shifted = send(tokens, [(a, a + 1, 0) for a in range(sections - 1)])
     held_out = jnp.where(section == 0, fresh_batches[TICKS - 1], shifted)
 

time: 324 us -> 338 us (1.043); the launches traced: 322 us -> 333 us
  blocking collectives: 16.2 us -> 28.1 us
  waiting for transfers between devices: 90.5 us -> 94.5 us
  local copies, waits for them, and re-layouts: 29.6 us -> 25.8 us
    all_to_all x1 -> x0, starting transfers between devices: 27.3 us -> none  [on_device(): lax.all_to_all(block, 'dp', split_axis=0, concat_axis=1, tiled=True)]
    ppermute x0 -> x7, starting transfers between devices: none -> 15.7 us  [on_device(): part = lax.ppermute(part, 'dp', [(d, d ^ mask) for d in range(ways)])]
    all_to_all x1, waiting for transfers between devices: 12 us -> 0.01 us  [on_device(): lax.all_to_all(received_grad, 'dp', split_axis=0, concat_axis=0, tiled=True)]
    all_gather x1, blocking collectives: 5.21 us -> 17 us  [on_device(): owner_grads = lax.all_gather(row_grad, 'section', axis=0, tiled=True)]
    ppermute x24, waiting for transfers between devices: 48.6 us -> 59.9 us  [send(): lax.ppermute(x, AXES, [(a * dps + i, b * dps + (i ^ flip)) for a, b, flip...]
    ppermute x0 -> x7, waiting for transfers between devices: none -> 10.7 us  [on_device(): part = lax.ppermute(part, 'dp', [(d, d ^ mask) for d in range(ways)])]
    all_to_all x1, starting transfers between devices: 3.64 us -> 12.7 us  [on_device(): lax.all_to_all(received_grad, 'dp', split_axis=0, concat_axis=0, tiled=True)]
    all_to_all x1 -> x0, waiting for transfers between devices: 6.43 us -> none  [on_device(): lax.all_to_all(block, 'dp', split_axis=0, concat_axis=1, tiled=True)]
  transfers between devices with their start and end apart: 31 -> 37, of which waited for: 15 -> 14; matrix products, arithmetic and copies ran while one was open for 23% -> 21% of each run, Pallas kernels for 0% -> 0%
where the time goes in v1:
time: 338 us; the launch traced here: 333 us
  starting transfers between devices  129 us (38%)
  waiting for transfers between devices  94.5 us (28%)
  matrix products  29.8 us (9%)
  blocking collectives  28.1 us (8%)
  local copies, waits for them, and re-layouts  25.8 us (8%)
  other arithmetic  24 us (7%)
    ppermute x24, starting transfers between devices, send(): lax.ppermute(x, AXES, [(a * dps + i, b * dps + (i ^ flip)) for a, b, flip...  70.7 us
    ppermute x24, waiting for transfers between devices, send(): lax.ppermute(x, AXES, [(a * dps + i, b * dps + (i ^ flip)) for a, b, flip...  59.9 us
    all_to_all x4, starting transfers between devices, spread(): lax.all_to_all(jnp.broadcast_to(x[None], (dps, *x.shape)), 'dp', split_ax...  24.1 us
    all_to_all x4, waiting for transfers between devices, spread(): lax.all_to_all(jnp.broadcast_to(x[None], (dps, *x.shape)), 'dp', split_ax...  23.9 us
    all_gather x1, blocking collectives, on_device(): owner_grads = lax.all_gather(row_grad, 'section', axis=0, tiled=True)  17 us
    ppermute x7, starting transfers between devices, on_device(): part = lax.ppermute(part, 'dp', [(d, d ^ mask) for d in range(ways)])  15.7 us
    all_to_all x1, starting transfers between devices, on_device(): lax.all_to_all(received_grad, 'dp', split_axis=0, concat_axis=0, tiled=True)  12.7 us
    ppermute x7, waiting for transfers between devices, on_device(): part = lax.ppermute(part, 'dp', [(d, d ^ mask) for d in range(ways)])  10.7 us
  transfers between devices with their start and end apart: 37, of which 14 were waited for; matrix products, arithmetic and copies ran while one was open for 21% of the time, Pallas kernels for 0%

profile of v1, /device:TPU:0, one launch (start us, length us, event | category | flops | bytes accessed | tf_op | source)
XLA Modules:
  0.0 333.0 jit_solution(4056253683199677501)
XLA Ops:
  3.9 7.3 %all-to-all-start.1 = ((bf16[8,2,2048]{2,1,0:T(2,128)(2,1)}), bf16[8,2,2048]{2,1,0:T(2,128)(2,1)S(1)}, u32[]{:S(2)}, u32[]{:S(2)}) async-start(bf16[8,2,2048]{2,1,0:T(2,128)(2,1)} %reshape.403), calls=%async_computation.1 | async-start | bytes 131072 | tf_op jit(solution)/shard_map/all_to_all | solution.py:134
  17.5 3.9 %collective-permute-start.6 = (bf16[4,512,512]{2,1,0:T(8,128)(2,1)}, bf16[4,512,512]{2,1,0:T(8,128)(2,1)}, u32[]{:S(2)}, u32[]{:S(2)}) collective-permute-start(bf16[4,512,512]{2,1,0:T(8,128)(2,1)} %get-tuple-element.18), channel_id=1, source_target_pairs={{0,1},{1,0},{2,3},{3,2},{4,5},{5,4},{6,7},{7,6},{8,9},{9,8},{10,11... | collective-permute-start | bytes 6291464 | tf_op jit(solution)/shard_map/ppermute | solution.py:38
  24.9 3.3 dynamic-slice_reduce_fusion.1
  40.9 6.0 %all-to-all-start.2 = ((bf16[8,4,512]{2,1,0:T(4,128)(2,1)}), bf16[8,4,512]{2,1,0:T(4,128)(2,1)S(1)}, u32[]{:S(2)}, u32[]{:S(2)}) async-start(bf16[8,4,512]{2,1,0:T(4,128)(2,1)} %broadcast_in_dim.123), calls=%async_computation.2 | async-start | bytes 65536 | tf_op jit(solution)/shard_map/all_to_all | solution.py:134
  46.9 23.0 %all-to-all-done.2 = bf16[8,4,512]{2,1,0:T(4,128)(2,1)S(1)} async-done(((bf16[8,4,512]{2,1,0:T(4,128)(2,1)}), bf16[8,4,512]{2,1,0:T(4,128)(2,1)S(1)}, u32[]{:S(2)}, u32[]{:S(2)}) %all-to-all-start.2) | async-done | bytes 32800 | tf_op jit(solution)/shard_map/all_to_all | solution.py:134
  77.2 5.7 %all-to-all-start.3 = ((bf16[8,4,512]{2,1,0:T(4,128)(2,1)}), bf16[8,4,512]{2,1,0:T(4,128)(2,1)S(1)}, u32[]{:S(2)}, u32[]{:S(2)}) async-start(bf16[8,4,512]{2,1,0:T(4,128)(2,1)} %broadcast_in_dim.124), calls=%async_computation.3 | async-start | bytes 65536 | tf_op jit(solution)/shard_map/all_to_all | solution.py:134
  82.9 5.8 %all_gather.15 = bf16[32,4096]{1,0:T(8,128)(2,1)S(1)} all-gather(bf16[8,4096]{1,0:T(8,128)(2,1)S(1)} %copy-done.10), channel_id=1, replica_groups=mesh['section'=4,'dp'=8] {'section'}, dimensions={0}, use_global_device_ids=true | all-gather | bytes 327680 | tf_op jit(solution)/shard_map/all_gather | solution.py:53
  92.8 5.2 %all-gather.1 = bf16[4,12,512]{2,1,0:T(8,128)(2,1)S(1)} all-gather(bf16[1,12,512]{2,1,0:T(8,128)(2,1)S(1)} %maximum_bitcast_fusion), channel_id=2, replica_groups=mesh['section'=4,'dp'=8] {'section'}, dimensions={0}, use_global_device_ids=true | all-gather | bytes 61440 | tf_op jit(solution)/shard_map/all_gather | solution.py:153
  98.7 5.1 %all-to-all-start.4 = ((bf16[8,12,512]{2,1,0:T(8,128)(2,1)}), bf16[8,12,512]{2,1,0:T(8,128)(2,1)S(1)}, u32[]{:S(2)}, u32[]{:S(2)}) async-start(bf16[8,12,512]{2,1,0:T(8,128)(2,1)} %broadcast_in_dim.126), calls=%async_computation.4 | async-start | bytes 262144 | tf_op jit(solution)/shard_map/all_to_all | solution.py:134
  105.0 3.9 %collective-permute-start.1 = (bf16[128,2048]{1,0:T(8,128)(2,1)S(1)}, bf16[128,2048]{1,0:T(8,128)(2,1)S(1)}, u32[]{:S(2)}, u32[]{:S(2)}) collective-permute-start(bf16[128,2048]{1,0:T(8,128)(2,1)S(1)} %maximum_select_fusion.2), channel_id=1, source_target_pairs={{0,2},{1,3},{2,0},{3,1},{4,6},{5,7},{6,4},{7,5},{16,18},{17,19},{1... | collective-permute-start | bytes 1572872 | tf_op jit(solution)/shard_map/ppermute | solution.py:38
  108.9 4.3 %collective-permute-start.2 = (bf16[128,2048]{1,0:T(8,128)(2,1)S(1)}, bf16[128,2048]{1,0:T(8,128)(2,1)S(1)}, u32[]{:S(2)}, u32[]{:S(2)}) collective-permute-start(bf16[128,2048]{1,0:T(8,128)(2,1)S(1)} %maximum_select_fusion.2), channel_id=1, source_target_pairs={{0,4},{1,5},{2,6},{3,7},{4,0},{5,1},{6,2},{7,3},{16,20},{17,21},{1... | collective-permute-start | bytes 1572872 | tf_op jit(solution)/shard_map/ppermute | solution.py:38
  115.1 6.0 %all-to-all-start = ((bf16[8,8,4224]{2,1,0:T(8,128)(2,1)}), bf16[8,8,4224]{2,1,0:T(8,128)(2,1)}, u32[]{:S(2)}, u32[]{:S(2)}) async-start(bf16[8,8,4224]{2,1,0:T(8,128)(2,1)} %pad_maximum_fusion.1), calls=%async_computation | async-start | bytes 1081344 | tf_op jit(solution)/shard_map/all_to_all | solution.py:52
  121.2 19.7 %collective-permute-done.2 = bf16[128,2048]{1,0:T(8,128)(2,1)S(1)} collective-permute-done((bf16[128,2048]{1,0:T(8,128)(2,1)S(1)}, bf16[128,2048]{1,0:T(8,128)(2,1)S(1)}, u32[]{:S(2)}, u32[]{:S(2)}) %collective-permute-start.2) | collective-permute-done | bytes 524320 | tf_op jit(solution)/shard_map/ppermute | solution.py:38
  144.0 3.6 %gather_fusion.2 = bf16[4,512,512]{2,1,0:T(8,128)(2,1)} fusion(bf16[4,512,512]{2,1,0:T(8,128)(2,1)} %collective-permute-done.6, s32[1024]{0:T(1024)S(1)} %pad_clamp_fusion.2), kind=kCustom, calls=%fused_computation.2.clone | custom fusion | bytes 4194320 | tf_op jit(solution)/shard_map/jit(_take)/gather | solution.py:65
  149.7 4.4 %convolution_convert_fusion.4 = bf16[512,512]{1,0:T(8,128)(2,1)S(1)} fusion(bf16[512,2048]{1,0:T(8,128)(2,1)} %get-tuple-element.16, bf16[2048,512]{1,0:T(8,128)(2,1)S(1)} %bitcast.204), kind=kOutput, calls=%fused_computation.46 | convolution fusion | flops 1074003968 | bytes 4718592 | tf_op jit(solution)/shard_map/dot_general | solution.py:79
  154.0 3.4 %collective-permute-start.7 = (bf16[512,512]{1,0:T(8,128)(2,1)S(1)}, bf16[512,512]{1,0:T(8,128)(2,1)S(1)}, u32[]{:S(2)}, u32[]{:S(2)}) collective-permute-start(bf16[512,512]{1,0:T(8,128)(2,1)S(1)} %convolution_convert_fusion.4), channel_id=1, source_target_pairs={{0,1},{1,0},{2,3},{3,2},{4,5},{5,4},{6,7},{7,6}} | collective-permute-start | bytes 1572872 | tf_op jit(solution)/shard_map/ppermute | solution.py:38
  159.9 5.2 %collective-permute-done.8 = f32[512]{0:T(512)S(1)} collective-permute-done((f32[512]{0:T(512)S(1)}, f32[512]{0:T(512)S(1)}, u32[]{:S(2)}, u32[]{:S(2)}) %collective-permute-start.8) | collective-permute-done | bytes 2080 | tf_op jit(solution)/shard_map/ppermute | solution.py:38
  175.1 7.4 %collective-permute-done.5 = bf16[512,2048]{1,0:T(8,128)(2,1)} collective-permute-done((bf16[512,2048]{1,0:T(8,128)(2,1)}, bf16[512,2048]{1,0:T(8,128)(2,1)}, u32[]{:S(2)}, u32[]{:S(2)}) %collective-permute-start.5) | collective-permute-done | bytes 2097184 | tf_op jit(solution)/shard_map/ppermute | solution.py:38
  183.8 4.5 %collective-permute-done.12 = bf16[512,512]{1,0:T(8,128)(2,1)S(1)} collective-permute-done((bf16[512,512]{1,0:T(8,128)(2,1)S(1)}, bf16[512,512]{1,0:T(8,128)(2,1)S(1)}, u32[]{:S(2)}, u32[]{:S(2)}) %collective-permute-start.12) | collective-permute-done | bytes 524320 | tf_op jit(solution)/shard_map/ppermute | solution.py:38
  192.7 3.4 %collective-permute-start.13 = (bf16[512,512]{1,0:T(8,128)(2,1)}, bf16[512,512]{1,0:T(8,128)(2,1)}, u32[]{:S(2)}, u32[]{:S(2)}) collective-permute-start(bf16[512,512]{1,0:T(8,128)(2,1)} %convolution_convert_fusion.3), channel_id=1, source_target_pairs={{0,1},{1,0},{2,3},{3,2},{4,5},{5,4},{6,7},{7,6},{8,9},{9,8},{10,11... | collective-permute-start | bytes 1572872 | tf_op jit(solution)/shard_map/ppermute | solution.py:38
  204.1 4.7 %add_convert_fusion.1 = bf16[512,512]{1,0:T(8,128)(2,1)} fusion(f32[512]{0:T(512)S(1)} %add_rsqrt_fusion.1, bf16[512,512]{1,0:T(8,128)(2,1)} %collective-permute-done.13, bf16[512,2048]{1,0:T(8,128)(2,1)} %copy-done.2, bf16[2048,512]{1,0:T(8,128)(2,1)} %bitcast.202, s32[]{:T(128)S(6)} %select_n.252), kind=kOutput, calls=%fused_computation.64 | convolution fusion | flops 1076887552 | bytes 5769220 | tf_op jit(solution)/shard_map/dot_general | solution.py:81
  212.5 9.0 %collective-permute-start.15 = (bf16[512,512]{1,0:T(8,128)(2,1)S(1)}, bf16[512,512]{1,0:T(8,128)(2,1)S(1)}, u32[]{:S(2)}, u32[]{:S(2)}) collective-permute-start(bf16[512,512]{1,0:T(8,128)(2,1)S(1)} %bitcast_select_fusion.2), channel_id=1, source_target_pairs={{0,8},{1,9},{2,10},{3,11},{4,12},{5,13},{6,14},{7,15},{8,16},{9,17... | collective-permute-start | bytes 1572872 | tf_op jit(solution)/shard_map/ppermute | solution.py:38
  221.5 13.5 %collective-permute-start.16 = (bf16[512,512]{1,0:T(8,128)(2,1)S(1)}, bf16[512,512]{1,0:T(8,128)(2,1)S(1)}, u32[]{:S(2)}, u32[]{:S(2)}) collective-permute-start(bf16[512,512]{1,0:T(8,128)(2,1)S(1)} %bitcast_select_fusion.2), channel_id=1, source_target_pairs={{0,10},{1,11},{2,8},{3,9},{4,14},{5,15},{6,12},{7,13},{8,18},{9,19... | collective-permute-start | bytes 1572872 | tf_op jit(solution)/shard_map/ppermute | solution.py:38
  238.5 7.8 %collective-permute-done.16 = bf16[512,512]{1,0:T(8,128)(2,1)S(1)} collective-permute-done((bf16[512,512]{1,0:T(8,128)(2,1)S(1)}, bf16[512,512]{1,0:T(8,128)(2,1)S(1)}, u32[]{:S(2)}, u32[]{:S(2)}) %collective-permute-start.16) | collective-permute-done | bytes 524320 | tf_op jit(solution)/shard_map/ppermute | solution.py:38
  246.3 5.7 %collective-permute-done.17 = bf16[512,512]{1,0:T(8,128)(2,1)S(1)} collective-permute-done((bf16[512,512]{1,0:T(8,128)(2,1)S(1)}, bf16[512,512]{1,0:T(8,128)(2,1)S(1)}, u32[]{:S(2)}, u32[]{:S(2)}) %collective-permute-start.17) | collective-permute-done | bytes 524320 | tf_op jit(solution)/shard_map/ppermute | solution.py:38
  251.9 5.7 %collective-permute-done.18 = bf16[512,512]{1,0:T(8,128)(2,1)S(1)} collective-permute-done((bf16[512,512]{1,0:T(8,128)(2,1)S(1)}, bf16[512,512]{1,0:T(8,128)(2,1)S(1)}, u32[]{:S(2)}, u32[]{:S(2)}) %collective-permute-start.18) | collective-permute-done | bytes 524320 | tf_op jit(solution)/shard_map/ppermute | solution.py:38
  259.9 3.4 %collective-permute-start.19 = (bf16[512,512]{1,0:T(8,128)(2,1)S(1)}, bf16[512,512]{1,0:T(8,128)(2,1)S(1)}, u32[]{:S(2)}, u32[]{:S(2)}) collective-permute-start(bf16[512,512]{1,0:T(8,128)(2,1)S(1)} %convolution_convert_fusion.2), channel_id=1, source_target_pairs={{0,1},{1,0},{2,3},{3,2},{4,5},{5,4},{6,7},{7,6},{8,9},{9,8},{10,11... | collective-permute-start | bytes 1572872 | tf_op jit(solution)/shard_map/ppermute | solution.py:38
  266.6 17.0 %all_gather.14 = f32[32,64]{1,0:T(8,128)S(1)} all-gather(f32[8,64]{1,0:T(8,128)S(1)} %select_reduce_fusion), channel_id=1, replica_groups=mesh['section'=4,'dp'=8] {'section'}, dimensions={0}, use_global_device_ids=true | all-gather | bytes 10240 | tf_op jit(solution)/shard_map/all_gather | solution.py:184
  289.1 12.7 %all-to-all-start.5 = ((bf16[8,8,4096]{2,1,0:T(8,128)(2,1)}), bf16[8,8,4096]{2,1,0:T(8,128)(2,1)S(1)}, u32[]{:S(2)}, u32[]{:S(2)}) async-start(bf16[8,8,4096]{2,1,0:T(8,128)(2,1)} %fusion.2), calls=%async_computation.5 | async-start | bytes 1048576 | tf_op jit(solution)/shard_map/all_to_all | solution.py:189
  307.7 3.8 %collective-permute-start.26 = (bf16[64,512]{1,0:T(8,128)(2,1)S(1)}, bf16[64,512]{1,0:T(8,128)(2,1)S(1)}, u32[]{:S(2)}, u32[]{:S(2)}) collective-permute-start(bf16[64,512]{1,0:T(8,128)(2,1)S(1)} %get-tuple-element.20), channel_id=1, source_target_pairs={{0,6},{1,7},{2,4},{3,5},{4,2},{5,3},{6,0},{7,1},{8,14},{9,15},{10,... | collective-permute-start | bytes 196616 | tf_op jit(solution)/shard_map/ppermute | solution.py:127
  313.3 4.4 %collective-permute-start.27 = (bf16[64,512]{1,0:T(8,128)(2,1)S(1)}, bf16[64,512]{1,0:T(8,128)(2,1)S(1)}, u32[]{:S(2)}, u32[]{:S(2)}) collective-permute-start(bf16[64,512]{1,0:T(8,128)(2,1)S(1)} %get-tuple-element.19), channel_id=1, source_target_pairs={{0,7},{1,6},{2,5},{3,4},{4,3},{5,2},{6,1},{7,0},{8,15},{9,14},{10,... | collective-permute-start | bytes 196616 | tf_op jit(solution)/shard_map/ppermute | solution.py:127
  317.8 6.9 %collective-permute-done.24 = bf16[64,512]{1,0:T(8,128)(2,1)S(1)} collective-permute-done((bf16[64,512]{1,0:T(8,128)(2,1)S(1)}, bf16[64,512]{1,0:T(8,128)(2,1)S(1)}, u32[]{:S(2)}, u32[]{:S(2)}) %collective-permute-start.24) | collective-permute-done | bytes 65568 | tf_op jit(solution)/shard_map/ppermute | solution.py:127
  (206 shorter events, 105.5 us)
Async XLA Ops:
  3.9 30.9 %all-to-all-start.1 = ((bf16[8,2,2048]{2,1,0:T(2,128)(2,1)}), bf16[8,2,2048]{2,1,0:T(2,128)(2,1)S(1)}, u32[]{:S(2)}, u32[]{:S(2)}) async-start(bf16[8,2,2048]{2,1,0:T(2,128)(2,1)} %reshape.403), calls=%async_computation.1 | async-start | bytes 131072 | tf_op jit(solution)/shard_map/all_to_all | solution.py:134
  17.5 126.5 %collective-permute-start.6 = (bf16[4,512,512]{2,1,0:T(8,128)(2,1)}, bf16[4,512,512]{2,1,0:T(8,128)(2,1)}, u32[]{:S(2)}, u32[]{:S(2)}) collective-permute-start(bf16[4,512,512]{2,1,0:T(8,128)(2,1)} %get-tuple-element.18), channel_id=1, source_target_pairs={{0,1},{1,0},{2,3},{3,2},{4,5},{5,4},{6,7},{7,6},{8,9},{9,8},{10,11... | collective-permute-start | bytes 6291464 | tf_op jit(solution)/shard_map/ppermute | solution.py:38
  29.0 74.8 %collective-permute-start = (bf16[64,2048]{1,0:T(8,128)(2,1)}, bf16[64,2048]{1,0:T(8,128)(2,1)}, u32[]{:S(2)}, u32[]{:S(2)}) collective-permute-start(bf16[64,2048]{1,0:T(8,128)(2,1)} %bitcast.53), channel_id=1, source_target_pairs={{0,1},{1,0},{2,3},{3,2},{4,5},{5,4},{6,7},{7,6},{16,17},{17,16},{1... | collective-permute-start | bytes 786440 | tf_op jit(solution)/shard_map/ppermute | solution.py:38
  40.9 29.0 %all-to-all-start.2 = ((bf16[8,4,512]{2,1,0:T(4,128)(2,1)}), bf16[8,4,512]{2,1,0:T(4,128)(2,1)S(1)}, u32[]{:S(2)}, u32[]{:S(2)}) async-start(bf16[8,4,512]{2,1,0:T(4,128)(2,1)} %broadcast_in_dim.123), calls=%async_computation.2 | async-start | bytes 65536 | tf_op jit(solution)/shard_map/all_to_all | solution.py:134
  77.2 12.4 %all-to-all-start.3 = ((bf16[8,4,512]{2,1,0:T(4,128)(2,1)}), bf16[8,4,512]{2,1,0:T(4,128)(2,1)S(1)}, u32[]{:S(2)}, u32[]{:S(2)}) async-start(bf16[8,4,512]{2,1,0:T(4,128)(2,1)} %broadcast_in_dim.124), calls=%async_computation.3 | async-start | bytes 65536 | tf_op jit(solution)/shard_map/all_to_all | solution.py:134
  98.7 16.4 %all-to-all-start.4 = ((bf16[8,12,512]{2,1,0:T(8,128)(2,1)}), bf16[8,12,512]{2,1,0:T(8,128)(2,1)S(1)}, u32[]{:S(2)}, u32[]{:S(2)}) async-start(bf16[8,12,512]{2,1,0:T(8,128)(2,1)} %broadcast_in_dim.126), calls=%async_computation.4 | async-start | bytes 262144 | tf_op jit(solution)/shard_map/all_to_all | solution.py:134
  105.0 16.2 %collective-permute-start.1 = (bf16[128,2048]{1,0:T(8,128)(2,1)S(1)}, bf16[128,2048]{1,0:T(8,128)(2,1)S(1)}, u32[]{:S(2)}, u32[]{:S(2)}) collective-permute-start(bf16[128,2048]{1,0:T(8,128)(2,1)S(1)} %maximum_select_fusion.2), channel_id=1, source_target_pairs={{0,2},{1,3},{2,0},{3,1},{4,6},{5,7},{6,4},{7,5},{16,18},{17,19},{1... | collective-permute-start | bytes 1572872 | tf_op jit(solution)/shard_map/ppermute | solution.py:38
  108.9 31.9 %collective-permute-start.2 = (bf16[128,2048]{1,0:T(8,128)(2,1)S(1)}, bf16[128,2048]{1,0:T(8,128)(2,1)S(1)}, u32[]{:S(2)}, u32[]{:S(2)}) collective-permute-start(bf16[128,2048]{1,0:T(8,128)(2,1)S(1)} %maximum_select_fusion.2), channel_id=1, source_target_pairs={{0,4},{1,5},{2,6},{3,7},{4,0},{5,1},{6,2},{7,3},{16,20},{17,21},{1... | collective-permute-start | bytes 1572872 | tf_op jit(solution)/shard_map/ppermute | solution.py:38
  113.2 27.7 %collective-permute-start.3 = (bf16[128,2048]{1,0:T(8,128)(2,1)S(1)}, bf16[128,2048]{1,0:T(8,128)(2,1)S(1)}, u32[]{:S(2)}, u32[]{:S(2)}) collective-permute-start(bf16[128,2048]{1,0:T(8,128)(2,1)S(1)} %maximum_select_fusion.2), channel_id=1, source_target_pairs={{0,6},{1,7},{2,4},{3,5},{4,2},{5,3},{6,0},{7,1},{16,22},{17,23},{1... | collective-permute-start | bytes 1572872 | tf_op jit(solution)/shard_map/ppermute | solution.py:38
  115.1 81.0 %all-to-all-start = ((bf16[8,8,4224]{2,1,0:T(8,128)(2,1)}), bf16[8,8,4224]{2,1,0:T(8,128)(2,1)}, u32[]{:S(2)}, u32[]{:S(2)}) async-start(bf16[8,8,4224]{2,1,0:T(8,128)(2,1)} %pad_maximum_fusion.1), calls=%async_computation | async-start | bytes 1081344 | tf_op jit(solution)/shard_map/all_to_all | solution.py:52
  142.4 40.1 %collective-permute-start.5 = (bf16[512,2048]{1,0:T(8,128)(2,1)}, bf16[512,2048]{1,0:T(8,128)(2,1)}, u32[]{:S(2)}, u32[]{:S(2)}) collective-permute-start(bf16[512,2048]{1,0:T(8,128)(2,1)} %get-tuple-element.16), channel_id=1, source_target_pairs={{16,0},{17,1},{18,2},{19,3},{20,4},{21,5},{22,6},{23,7}} | collective-permute-start | bytes 6291464 | tf_op jit(solution)/shard_map/ppermute | solution.py:38
  154.0 11.1 %collective-permute-start.7 = (bf16[512,512]{1,0:T(8,128)(2,1)S(1)}, bf16[512,512]{1,0:T(8,128)(2,1)S(1)}, u32[]{:S(2)}, u32[]{:S(2)}) collective-permute-start(bf16[512,512]{1,0:T(8,128)(2,1)S(1)} %convolution_convert_fusion.4), channel_id=1, source_target_pairs={{0,1},{1,0},{2,3},{3,2},{4,5},{5,4},{6,7},{7,6}} | collective-permute-start | bytes 1572872 | tf_op jit(solution)/shard_map/ppermute | solution.py:38
  169.1 14.7 %collective-permute-start.10 = (bf16[512,512]{1,0:T(8,128)(2,1)S(1)}, bf16[512,512]{1,0:T(8,128)(2,1)S(1)}, u32[]{:S(2)}, u32[]{:S(2)}) collective-permute-start(bf16[512,512]{1,0:T(8,128)(2,1)S(1)} %bitcast.210), channel_id=1, source_target_pairs={{0,10},{1,11},{2,8},{3,9},{4,14},{5,15},{6,12},{7,13}} | collective-permute-start | bytes 1572872 | tf_op jit(solution)/shard_map/ppermute | solution.py:38
  170.4 13.4 %collective-permute-start.11 = (bf16[512,512]{1,0:T(8,128)(2,1)S(1)}, bf16[512,512]{1,0:T(8,128)(2,1)S(1)}, u32[]{:S(2)}, u32[]{:S(2)}) collective-permute-start(bf16[512,512]{1,0:T(8,128)(2,1)S(1)} %bitcast.211), channel_id=1, source_target_pairs={{0,12},{1,13},{2,14},{3,15},{4,8},{5,9},{6,10},{7,11}} | collective-permute-start | bytes 1572872 | tf_op jit(solution)/shard_map/ppermute | solution.py:38
  171.8 16.6 %collective-permute-start.12 = (bf16[512,512]{1,0:T(8,128)(2,1)S(1)}, bf16[512,512]{1,0:T(8,128)(2,1)S(1)}, u32[]{:S(2)}, u32[]{:S(2)}) collective-permute-start(bf16[512,512]{1,0:T(8,128)(2,1)S(1)} %bitcast.212), channel_id=1, source_target_pairs={{0,14},{1,15},{2,12},{3,13},{4,10},{5,11},{6,8},{7,9}} | collective-permute-start | bytes 1572872 | tf_op jit(solution)/shard_map/ppermute | solution.py:38
  173.1 15.3 %collective-permute-start.9 = (bf16[512,512]{1,0:T(8,128)(2,1)S(1)}, bf16[512,512]{1,0:T(8,128)(2,1)S(1)}, u32[]{:S(2)}, u32[]{:S(2)}) collective-permute-start(bf16[512,512]{1,0:T(8,128)(2,1)S(1)} %bitcast.213), channel_id=1, source_target_pairs={{0,8},{1,9},{2,10},{3,11},{4,12},{5,13},{6,14},{7,15}} | collective-permute-start | bytes 1572872 | tf_op jit(solution)/shard_map/ppermute | solution.py:38
  182.5 55.9 %collective-permute-start.4 = (bf16[512,2048]{1,0:T(8,128)(2,1)}, bf16[512,2048]{1,0:T(8,128)(2,1)S(1)}, u32[]{:S(2)}, u32[]{:S(2)}) collective-permute-start(bf16[512,2048]{1,0:T(8,128)(2,1)} %get-tuple-element.16), channel_id=1, source_target_pairs={{24,0},{25,1},{26,2},{27,3},{28,4},{29,5},{30,6},{31,7}} | collective-permute-start | bytes 6291464 | tf_op jit(solution)/shard_map/ppermute | solution.py:38
  192.7 11.4 %collective-permute-start.13 = (bf16[512,512]{1,0:T(8,128)(2,1)}, bf16[512,512]{1,0:T(8,128)(2,1)}, u32[]{:S(2)}, u32[]{:S(2)}) collective-permute-start(bf16[512,512]{1,0:T(8,128)(2,1)} %convolution_convert_fusion.3), channel_id=1, source_target_pairs={{0,1},{1,0},{2,3},{3,2},{4,5},{5,4},{6,7},{7,6},{8,9},{9,8},{10,11... | collective-permute-start | bytes 1572872 | tf_op jit(solution)/shard_map/ppermute | solution.py:38
  212.5 25.9 %collective-permute-start.15 = (bf16[512,512]{1,0:T(8,128)(2,1)S(1)}, bf16[512,512]{1,0:T(8,128)(2,1)S(1)}, u32[]{:S(2)}, u32[]{:S(2)}) collective-permute-start(bf16[512,512]{1,0:T(8,128)(2,1)S(1)} %bitcast_select_fusion.2), channel_id=1, source_target_pairs={{0,8},{1,9},{2,10},{3,11},{4,12},{5,13},{6,14},{7,15},{8,16},{9,17... | collective-permute-start | bytes 1572872 | tf_op jit(solution)/shard_map/ppermute | solution.py:38
  221.5 24.8 %collective-permute-start.16 = (bf16[512,512]{1,0:T(8,128)(2,1)S(1)}, bf16[512,512]{1,0:T(8,128)(2,1)S(1)}, u32[]{:S(2)}, u32[]{:S(2)}) collective-permute-start(bf16[512,512]{1,0:T(8,128)(2,1)S(1)} %bitcast_select_fusion.2), channel_id=1, source_target_pairs={{0,10},{1,11},{2,8},{3,9},{4,14},{5,15},{6,12},{7,13},{8,18},{9,19... | collective-permute-start | bytes 1572872 | tf_op jit(solution)/shard_map/ppermute | solution.py:38
  235.1 16.9 %collective-permute-start.17 = (bf16[512,512]{1,0:T(8,128)(2,1)S(1)}, bf16[512,512]{1,0:T(8,128)(2,1)S(1)}, u32[]{:S(2)}, u32[]{:S(2)}) collective-permute-start(bf16[512,512]{1,0:T(8,128)(2,1)S(1)} %bitcast_select_fusion.2), channel_id=1, source_target_pairs={{0,12},{1,13},{2,14},{3,15},{4,8},{5,9},{6,10},{7,11},{8,20},{9,21... | collective-permute-start | bytes 1572872 | tf_op jit(solution)/shard_map/ppermute | solution.py:38
  236.4 21.2 %collective-permute-start.18 = (bf16[512,512]{1,0:T(8,128)(2,1)S(1)}, bf16[512,512]{1,0:T(8,128)(2,1)S(1)}, u32[]{:S(2)}, u32[]{:S(2)}) collective-permute-start(bf16[512,512]{1,0:T(8,128)(2,1)S(1)} %bitcast_select_fusion.2), channel_id=1, source_target_pairs={{0,14},{1,15},{2,12},{3,13},{4,10},{5,11},{6,8},{7,9},{8,22},{9,23... | collective-permute-start | bytes 1572872 | tf_op jit(solution)/shard_map/ppermute | solution.py:38
  259.9 23.8 %collective-permute-start.19 = (bf16[512,512]{1,0:T(8,128)(2,1)S(1)}, bf16[512,512]{1,0:T(8,128)(2,1)S(1)}, u32[]{:S(2)}, u32[]{:S(2)}) collective-permute-start(bf16[512,512]{1,0:T(8,128)(2,1)S(1)} %convolution_convert_fusion.2), channel_id=1, source_target_pairs={{0,1},{1,0},{2,3},{3,2},{4,5},{5,4},{6,7},{7,6},{8,9},{9,8},{10,11... | collective-permute-start | bytes 1572872 | tf_op jit(solution)/shard_map/ppermute | solution.py:38
  264.2 19.5 %collective-permute-start.20 = (f32[512]{0:T(512)S(1)}, f32[512]{0:T(512)S(1)}, u32[]{:S(2)}, u32[]{:S(2)}) collective-permute-start(f32[512]{0:T(512)S(1)} %get-tuple-element.11), channel_id=1, source_target_pairs={{0,1},{1,0},{2,3},{3,2},{4,5},{5,4},{6,7},{7,6},{8,9},{9,8},{10,11... | collective-permute-start | bytes 6152 | tf_op jit(solution)/shard_map/ppermute | solution.py:38
  286.1 21.6 %collective-permute-start.21 = (bf16[64,512]{1,0:T(8,128)(2,1)S(1)}, bf16[64,512]{1,0:T(8,128)(2,1)S(1)}, u32[]{:S(2)}, u32[]{:S(2)}) collective-permute-start(bf16[64,512]{1,0:T(8,128)(2,1)S(1)} %get-tuple-element.25), channel_id=1, source_target_pairs={{0,1},{1,0},{2,3},{3,2},{4,5},{5,4},{6,7},{7,6},{8,9},{9,8},{10,11... | collective-permute-start | bytes 196616 | tf_op jit(solution)/shard_map/ppermute | solution.py:127
  289.1 40.0 %all-to-all-start.5 = ((bf16[8,8,4096]{2,1,0:T(8,128)(2,1)}), bf16[8,8,4096]{2,1,0:T(8,128)(2,1)S(1)}, u32[]{:S(2)}, u32[]{:S(2)}) async-start(bf16[8,8,4096]{2,1,0:T(8,128)(2,1)} %fusion.2), calls=%async_computation.5 | async-start | bytes 1048576 | tf_op jit(solution)/shard_map/all_to_all | solution.py:189
  301.8 11.5 %collective-permute-start.22 = (bf16[64,512]{1,0:T(8,128)(2,1)S(1)}, bf16[64,512]{1,0:T(8,128)(2,1)S(1)}, u32[]{:S(2)}, u32[]{:S(2)}) collective-permute-start(bf16[64,512]{1,0:T(8,128)(2,1)S(1)} %get-tuple-element.24), channel_id=1, source_target_pairs={{0,2},{1,3},{2,0},{3,1},{4,6},{5,7},{6,4},{7,5},{8,10},{9,11},{10,... | collective-permute-start | bytes 196616 | tf_op jit(solution)/shard_map/ppermute | solution.py:127
  303.8 13.9 %collective-permute-start.23 = (bf16[64,512]{1,0:T(8,128)(2,1)S(1)}, bf16[64,512]{1,0:T(8,128)(2,1)S(1)}, u32[]{:S(2)}, u32[]{:S(2)}) collective-permute-start(bf16[64,512]{1,0:T(8,128)(2,1)S(1)} %get-tuple-element.23), channel_id=1, source_target_pairs={{0,3},{1,2},{2,1},{3,0},{4,7},{5,6},{6,5},{7,4},{8,11},{9,10},{10,... | collective-permute-start | bytes 196616 | tf_op jit(solution)/shard_map/ppermute | solution.py:127
  305.3 19.4 %collective-permute-start.24 = (bf16[64,512]{1,0:T(8,128)(2,1)S(1)}, bf16[64,512]{1,0:T(8,128)(2,1)S(1)}, u32[]{:S(2)}, u32[]{:S(2)}) collective-permute-start(bf16[64,512]{1,0:T(8,128)(2,1)S(1)} %get-tuple-element.22), channel_id=1, source_target_pairs={{0,4},{1,5},{2,6},{3,7},{4,0},{5,1},{6,2},{7,3},{8,12},{9,13},{10,... | collective-permute-start | bytes 196616 | tf_op jit(solution)/shard_map/ppermute | solution.py:127
  307.7 19.0 %collective-permute-start.25 = (bf16[64,512]{1,0:T(8,128)(2,1)S(1)}, bf16[64,512]{1,0:T(8,128)(2,1)S(1)}, u32[]{:S(2)}, u32[]{:S(2)}) collective-permute-start(bf16[64,512]{1,0:T(8,128)(2,1)S(1)} %get-tuple-element.21), channel_id=1, source_target_pairs={{0,5},{1,4},{2,7},{3,6},{4,1},{5,0},{6,3},{7,2},{8,13},{9,12},{10,... | collective-permute-start | bytes 196616 | tf_op jit(solution)/shard_map/ppermute | solution.py:127
  307.7 19.0 %collective-permute-start.26 = (bf16[64,512]{1,0:T(8,128)(2,1)S(1)}, bf16[64,512]{1,0:T(8,128)(2,1)S(1)}, u32[]{:S(2)}, u32[]{:S(2)}) collective-permute-start(bf16[64,512]{1,0:T(8,128)(2,1)S(1)} %get-tuple-element.20), channel_id=1, source_target_pairs={{0,6},{1,7},{2,4},{3,5},{4,2},{5,3},{6,0},{7,1},{8,14},{9,15},{10,... | collective-permute-start | bytes 196616 | tf_op jit(solution)/shard_map/ppermute | solution.py:127
  313.3 13.4 %collective-permute-start.27 = (bf16[64,512]{1,0:T(8,128)(2,1)S(1)}, bf16[64,512]{1,0:T(8,128)(2,1)S(1)}, u32[]{:S(2)}, u32[]{:S(2)}) collective-permute-start(bf16[64,512]{1,0:T(8,128)(2,1)S(1)} %get-tuple-element.19), channel_id=1, source_target_pairs={{0,7},{1,6},{2,5},{3,4},{4,3},{5,2},{6,1},{7,0},{8,15},{9,14},{10,... | collective-permute-start | bytes 196616 | tf_op jit(solution)/shard_map/ppermute | solution.py:127
  (21 other events, 205.2 us)
